TPU v7x, 128 devices: a whole 4x4x4 slice. The times are simulated.
128 devices in a mesh: dev: 128 (over x, y, z, core).
Axes of the slice: x: 4, y: 4, z: 4, core: 2. Of those that a mesh axis runs over, the one named last changes fastest.
Arguments:
- params: float32 [9, 131072], P(None, 'dev')
- moment: float32 [9, 131072], P(None, 'dev'), may hold values from -3 to 3
- second: float32 [9, 131072], P(None, 'dev'), may hold values from 0.05 to 1
- fetch_ids: int32 [128, 128, 8], P('dev'), may hold values from 0 to 1023
- seg_ids: int32 [512, 256], P('dev'), may hold values from 0 to 1023
- seg_count: int32 [512], P('dev'), may hold values from 1 to 256, 98304 in all
- seg_perm: int32 [512], replicated, may hold values from 0 to 511, as said below
- target: float32 [128, 3, 256], P('dev'), may hold values from 0 to 1
Outputs:
- image: float32 [128, 3, 256], P('dev')
- new_params: float32 [9, 131072], P(None, 'dev')
- new_moment: float32 [9, 131072], P(None, 'dev')
- new_second: float32 [9, 131072], P(None, 'dev')
Inputs may be any that keep to these rules, and one draw needn't show every extreme that they name: `seg_count`: segments that exceed their count hold unused slots; some segment is full. `seg_perm`: each number appears once.
All inputs are finite; a program needn't handle non-finite values. No bound on the sum of `seg_count` on one device may be relied on, other than what follows from the above.
Results may differ from a plain program's by a relative error of at most 0.0003.
Values sent between devices are 32-bit elements; how exact they have to be, the bound alone decides.
A program may use at most 192 MiB of HBM per device.

v0:
```python
import jax
import jax.numpy as jnp
from jax import lax
from jax.sharding import PartitionSpec as P

TILES_X = 8
KSEG = 4


def segment(par, count, tile):
    span = par.shape[1]
    pidx = jnp.arange(256, dtype=jnp.int32)
    fine_x = ((pidx % 16).astype(jnp.float32) + 0.5) / 16.0
    fine_y = ((pidx // 16).astype(jnp.float32) + 0.5) / 16.0
    pos_x = (tile % TILES_X).astype(jnp.float32) + fine_x
    pos_y = (tile // TILES_X).astype(jnp.float32) + fine_y
    steps = jnp.arange(span, dtype=jnp.int32)
    live = (steps < count).astype(jnp.float32)
    delta_x = pos_x[None, :] - par[0][:, None]
    delta_y = pos_y[None, :] - par[1][:, None]
    scale_a = jnp.exp(par[2])
    scale_c = jnp.exp(par[3])
    cross = 0.8 * jnp.tanh(par[4]) * scale_a * scale_c
    power = -0.5 * (
        (scale_a * scale_a)[:, None] * delta_x * delta_x
        + 2.0 * cross[:, None] * delta_x * delta_y
        + (scale_c * scale_c)[:, None] * delta_y * delta_y
    )
    alpha = (0.95 * jax.nn.sigmoid(par[5]) * live)[:, None] * jnp.exp(power)
    logt = jnp.log1p(-alpha)
    lower = (steps[:, None] > steps[None, :]).astype(jnp.float32)
    earlier = jnp.dot(lower, logt, precision=lax.Precision.HIGHEST)
    weight = jnp.exp(earlier) * alpha
    colour = jnp.dot(par[6:9], weight, precision=lax.Precision.HIGHEST)
    return (colour, jnp.sum(logt, axis=0))


def per_device(params, moment, second, fetch_ids, seg_ids, seg_count, seg_perm, target):
    ndev = lax.axis_size("dev")
    me = lax.axis_index("dev")
    nparam, owned = params.shape
    segs, span = seg_ids.shape
    tiles_dev = target.shape[0]
    pixels = target.shape[2]
    wanted = fetch_ids[0]
    cap = wanted.shape[1]
    received = lax.all_to_all(wanted, "dev", split_axis=0, concat_axis=0, tiled=True)
    buckets = jnp.take(params, received, axis=1)
    arrived = lax.all_to_all(buckets, "dev", split_axis=1, concat_axis=1, tiled=True)
    buffer = arrived.reshape(nparam, ndev * cap)
    first = me * segs
    own_perm = lax.dynamic_slice_in_dim(seg_perm, first, segs, 0)
    own_tile = own_perm // KSEG
    own_rank = own_perm % KSEG
    gathered_par = jnp.moveaxis(jnp.take(buffer, seg_ids, axis=1), 1, 0)

    def partials(values):
        return jax.vmap(segment)(values, seg_count, own_tile)

    (colours, logs), back = jax.vjp(partials, gathered_par)
    all_colours, all_logs, all_target = (
        lax.all_gather(colours, "dev", axis=0, tiled=True),
        lax.all_gather(logs, "dev", axis=0, tiled=True),
        lax.all_gather(target, "dev", axis=0, tiled=True),
    )
    total = all_logs.shape[0]
    ntiles = all_target.shape[0]
    tile_all = seg_perm // KSEG
    rank_all = seg_perm % KSEG
    same = tile_all[:, None] == tile_all[None, :]
    before = (same & (rank_all[None, :] < rank_all[:, None])).astype(jnp.float32)
    prefix = jnp.exp(jnp.dot(before, all_logs, precision=lax.Precision.HIGHEST))
    contrib = (prefix[:, None, :] * all_colours).reshape(total, 3 * pixels)
    onehot = (jnp.arange(ntiles, dtype=jnp.int32)[:, None] == tile_all[None, :]).astype(jnp.float32)
    image = jnp.dot(onehot, contrib, precision=lax.Precision.HIGHEST)
    misfit = image - all_target.reshape(ntiles, 3 * pixels)
    later = (
        (own_tile[:, None] == tile_all[None, :]) & (rank_all[None, :] > own_rank[:, None])
    ).astype(jnp.float32)
    behind = jnp.dot(later, contrib, precision=lax.Precision.HIGHEST).reshape(segs, 3, pixels)
    picker = (own_tile[:, None] == jnp.arange(ntiles, dtype=jnp.int32)[None, :]).astype(jnp.float32)
    error = jnp.dot(picker, misfit, precision=lax.Precision.HIGHEST).reshape(segs, 3, pixels)
    own_prefix = lax.dynamic_slice_in_dim(prefix, first, segs, 0)
    d_colour = own_prefix[:, None, :] * error
    d_log = jnp.sum(error * behind, axis=1)
    (d_par,) = back((d_colour, d_log))
    slot_grad = (
        jnp.zeros((nparam, ndev * cap), jnp.float32)
        .at[:, seg_ids.reshape(-1)]
        .add(jnp.moveaxis(d_par, 1, 0).reshape(nparam, segs * span))
    )
    returned = lax.all_to_all(
        slot_grad.reshape(nparam, ndev, cap), "dev", split_axis=1, concat_axis=1, tiled=True
    )
    grad = (
        jnp.zeros((nparam, owned), jnp.float32)
        .at[:, received.reshape(-1)]
        .add(returned.reshape(nparam, ndev * cap))
    )
    new_moment = 0.9 * moment + 0.1 * grad
    new_second = 0.99 * second + 0.01 * grad * grad
    new_params = params - 0.05 * new_moment / (jnp.sqrt(new_second) + 1e-08)
    my_image = lax.dynamic_slice_in_dim(image, me * tiles_dev, tiles_dev, 0).reshape(
        tiles_dev, 3, pixels
    )
    return (my_image, new_params, new_moment, new_second)


def solution(mesh):
    placed = (
        P(None, "dev"),
        P(None, "dev"),
        P(None, "dev"),
        P("dev", None, None),
        P("dev", None),
        P("dev"),
        P(),
        P("dev", None, None),
    )
    return jax.shard_map(
        per_device,
        mesh=mesh,
        in_specs=placed,
        out_specs=(P("dev", None, None), P(None, "dev"), P(None, "dev"), P(None, "dev")),
        check_vma=False,
    )
```

profile of v0, /device:TPU:1, one launch (start us, length us, event | category | flops | bytes accessed | tf_op | source)
XLA Modules:
  0.0 180.8 jit_solution(5734400977405865448)
XLA Ops:
  7.2 1.4 copy.73
  8.6 11.5 %all-to-all-start = ((s32[128,1,8]{2,1,0:T(1,128)}), s32[128,1,8]{2,1,0:T(1,128)S(1)}, u32[]{:S(2)}, u32[]{:S(2)}) async-start(s32[128,1,8]{2,1,0:T(1,128)} %bitcast), calls=%async_computation | async-start | bytes 131072 | tf_op jit(solution)/shard_map/all_to_all | solution.py:47
  23.1 1.1 copy.74
  24.2 5.2 %all-to-all-done = s32[128,1,8]{2,1,0:T(1,128)S(1)} async-done(((s32[128,1,8]{2,1,0:T(1,128)}), s32[128,1,8]{2,1,0:T(1,128)S(1)}, u32[]{:S(2)}, u32[]{:S(2)}) %all-to-all-start) | async-done | bytes 4128 | tf_op jit(solution)/shard_map/all_to_all | solution.py:47
  29.5 2.8 %gather_fusion = f32[1024,9]{1,0:T(8,128)S(1)} fusion(f32[9,1024]{0,1:T(8,128)S(1)} %copy.74, s32[1024]{0:T(1024)S(1)} %broadcast_clamp_fusion.1), kind=kCustom, calls=%fused_computation | custom fusion | bytes 77824 | tf_op jit(solution)/shard_map/jit(_take)/gather | solution.py:48
  32.4 1.0 fusion.43
  33.4 4.8 %all-to-all-start.1 = ((f32[9,128,8]{0,2,1:T(8,128)}), f32[9,128,8]{0,2,1:T(8,128)S(1)}, u32[]{:S(2)}, u32[]{:S(2)}) async-start(f32[9,128,8]{0,2,1:T(8,128)} %fusion.43), calls=%async_computation.1 | async-start | bytes 1048576 | tf_op jit(solution)/shard_map/all_to_all | solution.py:49
  38.2 13.5 %all-to-all-done.1 = f32[9,128,8]{0,2,1:T(8,128)S(1)} async-done(((f32[9,128,8]{0,2,1:T(8,128)}), f32[9,128,8]{0,2,1:T(8,128)S(1)}, u32[]{:S(2)}, u32[]{:S(2)}) %all-to-all-start.1) | async-done | bytes 36896 | tf_op jit(solution)/shard_map/all_to_all | solution.py:49
  51.7 2.8 %gather_fusion.1 = f32[1024,9]{1,0:T(8,128)S(1)} fusion(f32[9,1024]{0,1:T(8,128)S(1)} %bitcast.116, s32[1024]{0:T(1024)S(1)} %broadcast_clamp_fusion), kind=kCustom, calls=%fused_computation.1 | custom fusion | bytes 77824 | tf_op jit(solution)/shard_map/jit(_take)/gather | solution.py:55
  54.9 1.5 convolution_exponential_fusion
  56.4 2.1 %fusion.60 = f32[4,3,256]{2,1,0:T(4,128)} fusion(f32[256,4,256]{0,2,1:T(8,128)S(1)} %convolution_exponential_fusion, f32[4,256]{1,0:T(4,128)S(1)} %get-tuple-element.48, f32[4,256]{1,0:T(4,128)S(1)} %get-tuple-element.51, f32[4,256]{1,0:T(4,128)S(1)} %get-tuple-element.56, f32[4,256]{1,0:T(4,128)S(1)} %get-tuple-element.44, ...), kind=kOutput, calls=%fused_computation.86 | convolution fusion | flops 12845056 | bytes 1110016 | tf_op jit(solution)/shard_map/jvp(vmap())/dot_general | solution.py:34
  58.5 33.7 %all_gather.11 = f32[128,3,256]{2,1,0:T(4,128)S(1)} all-gather(f32[1,3,256]{2,1,0:T(4,128)S(1)} %copy.80), channel_id=1, replica_groups=mesh['dev'=128] {'dev'}, dimensions={0}, use_global_device_ids=true | all-gather | bytes 396288 | tf_op jit(solution)/shard_map/all_gather | solution.py:64
  94.1 1.0 log-plus-one_reduce_fusion
  95.2 35.5 %all-gather = f32[128,4,256]{2,1,0:T(4,128)S(1)} all-gather(f32[1,4,256]{2,1,0:T(4,128)S(1)} %bitcast.127), channel_id=1, replica_groups=mesh['dev'=128] {'dev'}, dimensions={0}, use_global_device_ids=true | all-gather | bytes 528384 | tf_op jit(solution)/shard_map/all_gather | solution.py:63
  131.9 1.8 %copy.79 = f32[512,3,256]{0,2,1:T(8,128)S(1)} copy(f32[512,3,256]{2,1,0:T(4,128)} %all-gather.3.cloned.1.call-done) | data formatting | bytes 3145728 | tf_op jit(solution)/shard_map/all_gather | solution.py:62
  133.9 1.0 fusion.66
  135.2 1.1 fusion.72
  136.3 1.2 fusion.59
  137.5 0.8 fusion.12
  138.3 3.0 %fusion.33 = (f32[4,256]{1,0:T(4,128)S(1)}, f32[4,256]{1,0:T(4,128)S(1)}, f32[4,256]{1,0:T(4,128)S(1)}, f32[4,256]{1,0:T(4,128)S(1)}, f32[4,256]{1,0:T(4,128)S(1)}, /*index=5*/f32[4,256]{1,0:T(4,128)S(1)}) fusion(f32[4,256]{1,0:T(4,128)S(1)} %get-tuple-element.51, f32[4,256]{1,0:T(4,128)S(1)} %get-tuple-element.56, f32[4,256]{1,0:T(4,128)S(1)} %get-tuple-element.48, ...), kind=kOutput, calls=%fused_computation.52 | convolution fusion | flops 820570112 | bytes 2183168 | tf_op jit(solution)/shard_map/transpose(jvp(vmap()))/dot_general | solution.py:32
  141.9 6.8 %scatter_custom_fusion = f32[9,1024]{0,1:T(8,128)} fusion(s32[1024]{0:T(1024)S(1)} %bitcast.130, f32[1024,9]{1,0:T(8,128)S(1)} %copy.87, f32[]{:T(128)} %constant.149.clone.1), kind=kCustom, calls=%fused_computation.90 | custom fusion | flops 9216 | bytes 36868 | tf_op jit(solution)/shard_map/scatter-add | solution.py:90
  148.7 4.6 %all-to-all-start.2 = ((f32[9,128,8]{0,2,1:T(8,128)}), f32[9,128,8]{0,2,1:T(8,128)S(1)}, u32[]{:S(2)}, u32[]{:S(2)}) async-start(f32[9,128,8]{0,2,1:T(8,128)} %bitcast.30), calls=%async_computation.2 | async-start | bytes 1048576 | tf_op jit(solution)/shard_map/all_to_all | solution.py:92
  154.0 13.0 %all-to-all-done.2 = f32[9,128,8]{0,2,1:T(8,128)S(1)} async-done(((f32[9,128,8]{0,2,1:T(8,128)}), f32[9,128,8]{0,2,1:T(8,128)S(1)}, u32[]{:S(2)}, u32[]{:S(2)}) %all-to-all-start.2) | async-done | bytes 36896 | tf_op jit(solution)/shard_map/all_to_all | solution.py:92
  166.9 6.2 %scatter_custom_fusion.1 = f32[9,1024]{0,1:T(8,128)S(1)} fusion(s32[1024]{0:T(1024)S(1)} %bitcast.129, f32[9,128,8]{0,2,1:T(8,128)S(1)} %all-to-all-done.2, f32[]{:T(128)} %constant.149.clone.1), kind=kCustom, calls=%fused_computation.67 | custom fusion | flops 9216 | bytes 561156 | tf_op jit(solution)/shard_map/scatter-add | solution.py:98
  (74 shorter events, 9.0 us)
Async XLA Ops:
  8.6 20.8 %all-to-all-start = ((s32[128,1,8]{2,1,0:T(1,128)}), s32[128,1,8]{2,1,0:T(1,128)S(1)}, u32[]{:S(2)}, u32[]{:S(2)}) async-start(s32[128,1,8]{2,1,0:T(1,128)} %bitcast), calls=%async_computation | async-start | bytes 131072 | tf_op jit(solution)/shard_map/all_to_all | solution.py:47
  32.3 22.4 %copy-start.6 = (s32[4]{0:T(128)S(1)}, s32[4]{0:T(128)}, u32[]{:S(2)}) copy-start(s32[4]{0:T(128)} %param.13) | copy-start | bytes 52
  33.4 18.3 %all-to-all-start.1 = ((f32[9,128,8]{0,2,1:T(8,128)}), f32[9,128,8]{0,2,1:T(8,128)S(1)}, u32[]{:S(2)}, u32[]{:S(2)}) async-start(f32[9,128,8]{0,2,1:T(8,128)} %fusion.43), calls=%async_computation.1 | async-start | bytes 1048576 | tf_op jit(solution)/shard_map/all_to_all | solution.py:49
  38.1 93.7 %all-gather.3.cloned.1.call-start = ((), (), s32[]{:S(2)}) async-start(), calls=%async_computation.3 | async-start | bytes 2113536 | tf_op jit(solution)/shard_map/all_gather | solution.py:62
  56.3 2.1 %copy-start.7 = (f32[256,4,256]{0,2,1:T(8,128)}, f32[256,4,256]{0,2,1:T(8,128)S(1)}, u32[]{:S(2)}) copy-start(f32[256,4,256]{0,2,1:T(8,128)S(1)} %convolution_exponential_fusion) | copy-start | bytes 3145732
  56.3 2.2 %copy-start.3 = (s32[4,256]{1,0:T(4,128)S(1)}, s32[4,256]{1,0:T(4,128)}, u32[]{:S(2)}) copy-start(s32[4,256]{1,0:T(4,128)} %param.12) | copy-start | bytes 12292
  56.4 2.2 %copy-start.5 = (f32[1,3,256]{2,0,1:T(1,128)S(1)}, f32[1,3,256]{2,0,1:T(1,128)}, u32[]{:S(2)}) copy-start(f32[1,3,256]{2,0,1:T(1,128)} %param.15) | copy-start | bytes 9220
  58.5 34.2 %copy-start.4 = (s32[512]{0:T(512)S(1)}, s32[512]{0:T(512)}, u32[]{:S(2)}) copy-start(s32[512]{0:T(512)} %param.14) | copy-start | bytes 6148
  133.9 2.4 %copy-start.8 = (f32[256,4,256]{0,2,1:T(8,128)S(1)}, f32[256,4,256]{0,2,1:T(8,128)}, u32[]{:S(2)}) copy-start(f32[256,4,256]{0,2,1:T(8,128)} %copy-done.7) | copy-start | bytes 3145732
  141.9 31.4 %copy-start = (f32[9,1024]{1,0:T(8,128)S(1)}, f32[9,1024]{1,0:T(8,128)}, u32[]{:S(2)}) copy-start(f32[9,1024]{1,0:T(8,128)} %param.8) | copy-start | bytes 110596
  141.9 31.4 %copy-start.1 = (f32[9,1024]{1,0:T(8,128)S(1)}, f32[9,1024]{1,0:T(8,128)}, u32[]{:S(2)}) copy-start(f32[9,1024]{1,0:T(8,128)} %param.9) | copy-start | bytes 110596
  141.9 31.4 %copy-start.2 = (f32[9,1024]{1,0:T(8,128)S(1)}, f32[9,1024]{1,0:T(8,128)}, u32[]{:S(2)}) copy-start(f32[9,1024]{1,0:T(8,128)} %param.10) | copy-start | bytes 110596
  148.7 18.2 %all-to-all-start.2 = ((f32[9,128,8]{0,2,1:T(8,128)}), f32[9,128,8]{0,2,1:T(8,128)S(1)}, u32[]{:S(2)}, u32[]{:S(2)}) async-start(f32[9,128,8]{0,2,1:T(8,128)} %bitcast.30), calls=%async_computation.2 | async-start | bytes 1048576 | tf_op jit(solution)/shard_map/all_to_all | solution.py:92
Sparse Core Ops, SparseCore 0:
  58.6 62.3 all-gather.2
where the time goes:
time: 181 us
  blocking collectives  69.2 us (38%)
  waiting for transfers between devices  31.7 us (18%)
  starting transfers between devices  20.9 us (12%)
  other arithmetic  20.1 us (11%)
  between operations  14.5 us (8%)
  local copies, waits for them, and re-layouts  12.7 us (7%)
  matrix products  11.7 us (6%)
    all_gather x1, blocking collectives, per_device(): lax.all_gather(logs, 'dev', axis=0, tiled=True)  35.5 us
    all_gather x1, blocking collectives, per_device(): lax.all_gather(target, 'dev', axis=0, tiled=True)  33.7 us
    all_to_all x1, waiting for transfers between devices, per_device(): lax.all_to_all(buckets, 'dev', split_axis=1, concat_axis=1, tiled=True)  13.5 us
    all_to_all x1, waiting for transfers between devices, per_device(): lax.all_to_all(slot_grad.reshape(nparam, ndev, cap), 'dev', split_axis=1,...  13 us
    all_to_all x1, starting transfers between devices, per_device(): lax.all_to_all(wanted, 'dev', split_axis=0, concat_axis=0, tiled=True)  11.5 us
    scatter-add x1, other arithmetic, per_device(): slot_grad = jnp.zeros((nparam, ndev * cap), jnp.float32).at[:, seg_ids.re...  6.79 us
    scatter-add x1, other arithmetic, per_device(): grad = jnp.zeros((nparam, owned), jnp.float32).at[:, received.reshape(-1)...  6.18 us
    all_to_all x1, waiting for transfers between devices, per_device(): lax.all_to_all(wanted, 'dev', split_axis=0, concat_axis=0, tiled=True)  5.21 us
  transfers between devices with their start and end apart: 4, of which 3 were waited for; matrix products, arithmetic and copies ran while one was open for 5% of the time, Pallas kernels for 0%

commit v1 on v0

--- a/solution.py
+++ b/solution.py
@@ -46,7 +46,10 @@
     cap = wanted.shape[1]
     received = lax.all_to_all(wanted, "dev", split_axis=0, concat_axis=0, tiled=True)
     buckets = jnp.take(params, received, axis=1)
-    arrived = lax.all_to_all(buckets, "dev", split_axis=1, concat_axis=1, tiled=True)
+    arrived = jnp.concatenate(
+        lax.all_to_all(jnp.stack(jnp.split(buckets, lax.axis_size("dev"), axis=1)), "dev", 0, 0),
+        axis=1,
+    )
     buffer = arrived.reshape(nparam, ndev * cap)
     first = me * segs
     own_perm = lax.dynamic_slice_in_dim(seg_perm, first, segs, 0)

time: 181 us -> 256 us (1.41)
  local copies, waits for them, and re-layouts: 12.7 us -> 88.3 us
    unnamed x27 -> x154, local copies, waits for them, and re-layouts: 2.74 us -> 77.7 us
  transfers between devices with their start and end apart: 4 -> 4, of which waited for: 3 -> 3; matrix products, arithmetic and copies ran while one was open for 5% -> 3% of each run, Pallas kernels for 0% -> 0%
where the time goes in v1:
time: 256 us
  local copies, waits for them, and re-layouts  88.3 us (34%)
  blocking collectives  69.2 us (27%)
  waiting for transfers between devices  31.7 us (12%)
  starting transfers between devices  20.9 us (8%)
  other arithmetic  19.3 us (8%)
  between operations  14.6 us (6%)
  matrix products  11.7 us (5%)
    unnamed x154, local copies, waits for them, and re-layouts  77.7 us
    all_gather x1, blocking collectives, per_device(): lax.all_gather(logs, 'dev', axis=0, tiled=True)  35.5 us
    all_gather x1, blocking collectives, per_device(): lax.all_gather(target, 'dev', axis=0, tiled=True)  33.7 us
    all_to_all x1, waiting for transfers between devices, per_device(): lax.all_to_all(jnp.stack(jnp.split(buckets, lax.axis_size('dev'), axis=1)...  13.5 us
    all_to_all x1, waiting for transfers between devices, per_device(): lax.all_to_all(slot_grad.reshape(nparam, ndev, cap), 'dev', split_axis=1,...  13 us
    all_to_all x1, starting transfers between devices, per_device(): lax.all_to_all(wanted, 'dev', split_axis=0, concat_axis=0, tiled=True)  11.5 us
    scatter-add x1, other arithmetic, per_device(): slot_grad = jnp.zeros((nparam, ndev * cap), jnp.float32).at[:, seg_ids.re...  6.79 us
    scatter-add x1, other arithmetic, per_device(): grad = jnp.zeros((nparam, owned), jnp.float32).at[:, received.reshape(-1)...  6.18 us
  transfers between devices with their start and end apart: 4, of which 3 were waited for; matrix products, arithmetic and copies ran while one was open for 3% of the time, Pallas kernels for 0%

profile of v1, /device:TPU:1, one launch (start us, length us, event | category | flops | bytes accessed | tf_op | source)
XLA Modules:
  0.0 255.7 jit_solution(10693653764617691195)
XLA Ops:
  7.2 1.4 copy.530
  8.6 11.5 %all-to-all-start = ((s32[128,1,8]{2,1,0:T(1,128)}), s32[128,1,8]{2,1,0:T(1,128)S(1)}, u32[]{:S(2)}, u32[]{:S(2)}) async-start(s32[128,1,8]{2,1,0:T(1,128)} %bitcast), calls=%async_computation | async-start | bytes 131072 | tf_op jit(solution)/shard_map/all_to_all | solution.py:47
  23.1 1.1 copy.531
  24.2 5.2 %all-to-all-done = s32[128,1,8]{2,1,0:T(1,128)S(1)} async-done(((s32[128,1,8]{2,1,0:T(1,128)}), s32[128,1,8]{2,1,0:T(1,128)S(1)}, u32[]{:S(2)}, u32[]{:S(2)}) %all-to-all-start) | async-done | bytes 4128 | tf_op jit(solution)/shard_map/all_to_all | solution.py:47
  29.5 2.8 %gather_fusion = f32[1024,9]{1,0:T(8,128)S(1)} fusion(f32[9,1024]{0,1:T(8,128)S(1)} %copy.531, s32[1024]{0:T(1024)S(1)} %broadcast_clamp_fusion.1), kind=kCustom, calls=%fused_computation | custom fusion | bytes 77824 | tf_op jit(solution)/shard_map/jit(_take)/gather | solution.py:48
  108.2 4.8 %all-to-all-start.1 = ((f32[128,9,1,8]{1,3,2,0:T(8,128)}), f32[128,9,1,8]{1,3,2,0:T(8,128)S(1)}, u32[]{:S(2)}, u32[]{:S(2)}) async-start(f32[128,9,1,8]{1,3,2,0:T(8,128)} %constant_dynamic-update-slice_fusion), calls=%async_computation.1 | async-start | bytes 1048576 | tf_op jit(solution)/shard_map/all_to_all | solution.py:50
  113.0 13.5 %all-to-all-done.1 = f32[128,9,1,8]{1,3,2,0:T(8,128)S(1)} async-done(((f32[128,9,1,8]{1,3,2,0:T(8,128)}), f32[128,9,1,8]{1,3,2,0:T(8,128)S(1)}, u32[]{:S(2)}, u32[]{:S(2)}) %all-to-all-start.1) | async-done | bytes 36896 | tf_op jit(solution)/shard_map/all_to_all | solution.py:50
  126.5 2.8 %gather_fusion.1 = f32[1024,9]{1,0:T(8,128)S(1)} fusion(f32[9,1024]{0,1:T(8,128)S(1)} %bitcast.630, s32[1024]{0:T(1024)S(1)} %broadcast_clamp_fusion), kind=kCustom, calls=%fused_computation.1 | custom fusion | bytes 77824 | tf_op jit(solution)/shard_map/jit(_take)/gather | solution.py:58
  129.7 1.5 convolution_exponential_fusion
  131.2 2.1 fusion.60
  133.4 33.7 %all_gather.11 = f32[128,3,256]{2,1,0:T(4,128)S(1)} all-gather(f32[1,3,256]{2,1,0:T(4,128)S(1)} %copy.537), channel_id=1, replica_groups=mesh['dev'=128] {'dev'}, dimensions={0}, use_global_device_ids=true | all-gather | bytes 396288 | tf_op jit(solution)/shard_map/all_gather | solution.py:67
  168.1 0.8 reduce.3
  169.0 1.0 log-plus-one_reduce_fusion
  170.0 35.5 %all-gather = f32[128,4,256]{2,1,0:T(4,128)S(1)} all-gather(f32[1,4,256]{2,1,0:T(4,128)S(1)} %bitcast.641), channel_id=1, replica_groups=mesh['dev'=128] {'dev'}, dimensions={0}, use_global_device_ids=true | all-gather | bytes 528384 | tf_op jit(solution)/shard_map/all_gather | solution.py:66
  206.7 1.8 copy.536
  208.8 1.0 fusion.66
  210.1 1.1 fusion.72
  211.2 1.2 fusion.59
  212.3 0.8 fusion.12
  213.2 3.0 %fusion.33 = (f32[4,256]{1,0:T(4,128)S(1)}, f32[4,256]{1,0:T(4,128)S(1)}, f32[4,256]{1,0:T(4,128)S(1)}, f32[4,256]{1,0:T(4,128)S(1)}, f32[4,256]{1,0:T(4,128)S(1)}, /*index=5*/f32[4,256]{1,0:T(4,128)S(1)}) fusion(f32[4,256]{1,0:T(4,128)S(1)} %get-tuple-element.63, f32[4,256]{1,0:T(4,128)S(1)} %get-tuple-element.68, f32[4,256]{1,0:T(4,128)S(1)} %get-tuple-element.60, ...), kind=kOutput, calls=%fused_computation.52 | convolution fusion | flops 820570112 | bytes 2183168 | tf_op jit(solution)/shard_map/transpose(jvp(vmap()))/dot_general | solution.py:32
  216.8 6.8 %scatter_custom_fusion = f32[9,1024]{0,1:T(8,128)} fusion(s32[1024]{0:T(1024)S(1)} %bitcast.644, f32[1024,9]{1,0:T(8,128)S(1)} %copy.544, f32[]{:T(128)} %constant.149.clone.1), kind=kCustom, calls=%fused_computation.218 | custom fusion | flops 9216 | bytes 36868 | tf_op jit(solution)/shard_map/scatter-add | solution.py:93
  223.6 4.6 %all-to-all-start.2 = ((f32[9,128,8]{0,2,1:T(8,128)}), f32[9,128,8]{0,2,1:T(8,128)S(1)}, u32[]{:S(2)}, u32[]{:S(2)}) async-start(f32[9,128,8]{0,2,1:T(8,128)} %bitcast.159), calls=%async_computation.2 | async-start | bytes 1048576 | tf_op jit(solution)/shard_map/all_to_all | solution.py:95
  228.8 13.0 %all-to-all-done.2 = f32[9,128,8]{0,2,1:T(8,128)S(1)} async-done(((f32[9,128,8]{0,2,1:T(8,128)}), f32[9,128,8]{0,2,1:T(8,128)S(1)}, u32[]{:S(2)}, u32[]{:S(2)}) %all-to-all-start.2) | async-done | bytes 36896 | tf_op jit(solution)/shard_map/all_to_all | solution.py:95
  241.8 6.2 %scatter_custom_fusion.1 = f32[9,1024]{0,1:T(8,128)S(1)} fusion(s32[1024]{0:T(1024)S(1)} %bitcast.643, f32[9,128,8]{0,2,1:T(8,128)S(1)} %all-to-all-done.2, f32[]{:T(128)} %constant.149.clone.1), kind=kCustom, calls=%fused_computation.67 | custom fusion | flops 9216 | bytes 561156 | tf_op jit(solution)/shard_map/scatter-add | solution.py:101
  (202 shorter events, 84.0 us)
Async XLA Ops:
  8.6 20.8 %all-to-all-start = ((s32[128,1,8]{2,1,0:T(1,128)}), s32[128,1,8]{2,1,0:T(1,128)S(1)}, u32[]{:S(2)}, u32[]{:S(2)}) async-start(s32[128,1,8]{2,1,0:T(1,128)} %bitcast), calls=%async_computation | async-start | bytes 131072 | tf_op jit(solution)/shard_map/all_to_all | solution.py:47
  42.6 87.0 %copy-start.6 = (s32[4]{0:T(128)S(1)}, s32[4]{0:T(128)}, u32[]{:S(2)}) copy-start(s32[4]{0:T(128)} %param.13) | copy-start | bytes 52
  108.2 18.3 %all-to-all-start.1 = ((f32[128,9,1,8]{1,3,2,0:T(8,128)}), f32[128,9,1,8]{1,3,2,0:T(8,128)S(1)}, u32[]{:S(2)}, u32[]{:S(2)}) async-start(f32[128,9,1,8]{1,3,2,0:T(8,128)} %constant_dynamic-update-slice_fusion), calls=%async_computation.1 | async-start | bytes 1048576 | tf_op jit(solution)/shard_map/all_to_all | solution.py:50
  113.0 93.7 %all-gather.3.cloned.1.call-start = ((), (), s32[]{:S(2)}) async-start(), calls=%async_computation.3 | async-start | bytes 2113536 | tf_op jit(solution)/shard_map/all_gather | solution.py:65
  131.2 2.1 copy-start.7
  131.2 2.2 copy-start.3
  131.2 2.2 copy-start.5
  133.3 34.2 %copy-start.4 = (s32[512]{0:T(512)S(1)}, s32[512]{0:T(512)}, u32[]{:S(2)}) copy-start(s32[512]{0:T(512)} %param.14) | copy-start | bytes 6148
  208.8 2.4 copy-start.8
  216.8 31.4 %copy-start = (f32[9,1024]{1,0:T(8,128)S(1)}, f32[9,1024]{1,0:T(8,128)}, u32[]{:S(2)}) copy-start(f32[9,1024]{1,0:T(8,128)} %param.8) | copy-start | bytes 110596
  216.8 31.4 %copy-start.1 = (f32[9,1024]{1,0:T(8,128)S(1)}, f32[9,1024]{1,0:T(8,128)}, u32[]{:S(2)}) copy-start(f32[9,1024]{1,0:T(8,128)} %param.9) | copy-start | bytes 110596
  216.8 31.4 %copy-start.2 = (f32[9,1024]{1,0:T(8,128)S(1)}, f32[9,1024]{1,0:T(8,128)}, u32[]{:S(2)}) copy-start(f32[9,1024]{1,0:T(8,128)} %param.10) | copy-start | bytes 110596
  223.6 18.2 %all-to-all-start.2 = ((f32[9,128,8]{0,2,1:T(8,128)}), f32[9,128,8]{0,2,1:T(8,128)S(1)}, u32[]{:S(2)}, u32[]{:S(2)}) async-start(f32[9,128,8]{0,2,1:T(8,128)} %bitcast.159), calls=%async_computation.2 | async-start | bytes 1048576 | tf_op jit(solution)/shard_map/all_to_all | solution.py:95
Sparse Core Ops, SparseCore 0:
  133.5 62.3 all-gather.2
